TPU v7x, 512 devices: a whole 4x8x8 slice. The times are simulated.
512 devices in a mesh: ops: 8 (over x, core), sec: 64 (over z, y).
Axes of the slice: x: 4, y: 8, z: 8, core: 2. Of those that a mesh axis runs over, the one named last changes fastest.
Arguments:
- wavefunction: bfloat16 [256, 16, 128, 128], P('sec'), may hold values from -6 to 6
- left_ops: bfloat16 [32, 256, 128, 128], P('ops', 'sec'), may hold values from -0.5 to 0.5
- right_ops: bfloat16 [32, 256, 128, 128], P('ops', 'sec'), may hold values from -0.5 to 0.5
- site_weights: float32 [32, 16], P('ops'), may hold values from -1 to 1
- right_sector: int32 [256, 16], replicated, may hold values from 0 to 255, as said below
- left_dims: int32 [256], replicated, may hold values from 32 to 128
- right_dims: int32 [256], replicated, may hold values from 32 to 128
- basis: bfloat16 [4, 256, 16, 128, 128], P(None, 'sec', None, 'ops')
Outputs:
- sigma: bfloat16 [256, 16, 128, 128], P('sec', None, 'ops')
- correlations: float32 [4], replicated
Inputs may be any that keep to these rules, and one draw needn't show every extreme that they name: For each two-site state, right_sector maps the 256 left sectors one to one onto the 256 right sectors. Right sector r lies on index r // 4 of sec and left sector a on index a // 4; the slabs of one index of sec go to every index of sec, 1 slabs to each.
All inputs are finite; a program needn't handle non-finite values.
Results may differ from a plain program's by a relative error of at most 0.0055.
Values may be sent and summed in bfloat16 or wider, within the bound.
A program may use at most 128 MiB of HBM per device.

v0:
```python
import jax
import jax.numpy as jnp
from jax import lax
from jax.sharding import PartitionSpec as P


def lookup(values_table, positions):
    flattened = values_table.reshape(-1)
    matches = positions[..., None] == jnp.arange(flattened.shape[0], dtype=jnp.int32)
    return jnp.sum(jnp.where(matches, flattened, 0), axis=-1)


def per_device(
    wavefunction, left_ops, right_ops, site_weights, right_sector, left_dims, right_dims, basis
):
    sectors, state_count, block_width, _ = wavefunction.shape
    term_count = left_ops.shape[0]
    peers = lax.axis_size("sec")
    position = lax.axis_index("sec")
    sector_total = right_sector.shape[0]
    item_count = sectors * state_count
    capacity = item_count // peers
    slot_count = peers * capacity
    target_dev = (right_sector // sectors).reshape(peers, item_count)
    devices = jnp.arange(peers, dtype=jnp.int32)
    onehot = (target_dev[:, :, None] == devices[None, None, :]).astype(jnp.int32)
    earlier = jnp.cumsum(onehot, axis=1) - onehot
    rank_all = jnp.sum(earlier * onehot, axis=2)
    my_target = lax.dynamic_index_in_dim(target_dev, position, 0, keepdims=False)
    my_rank = lax.dynamic_index_in_dim(rank_all, position, 0, keepdims=False)
    my_slot = my_target * capacity + my_rank
    slot_match = my_slot[:, None] == jnp.arange(slot_count, dtype=jnp.int32)[None, :]
    source_item = jnp.sum(
        jnp.where(slot_match, jnp.arange(item_count, dtype=jnp.int32)[:, None], 0), axis=0
    )
    slot_used = jnp.any(slot_match, axis=0)
    indices = jnp.arange(block_width, dtype=jnp.int32)
    my_sectors = lax.dynamic_slice_in_dim(right_sector, position * sectors, sectors, 0)
    my_left_dims = lax.dynamic_slice_in_dim(left_dims, position * sectors, sectors, 0)
    paired_dims = lookup(right_dims, my_sectors)
    keep_mask = (indices[None, None, :, None] < my_left_dims[:, None, None, None]) & (
        indices[None, None, None, :] < paired_dims[:, :, None, None]
    )
    masked = jnp.where(keep_mask, wavefunction, jnp.zeros_like(wavefunction))
    owned = position * sectors + jnp.arange(sectors, dtype=jnp.int32)
    matches_right = right_sector[None, :, :] == owned[:, None, None]
    anchor = jnp.sum(
        jnp.where(matches_right, jnp.arange(sector_total, dtype=jnp.int32)[None, :, None], 0),
        axis=1,
    )
    anchor_dev = anchor // sectors
    anchor_item = anchor % sectors * state_count + jnp.arange(state_count, dtype=jnp.int32)[None, :]
    anchor_rank = lookup(rank_all, anchor_dev * item_count + anchor_item)
    gather_rows = (anchor_dev * capacity + anchor_rank).reshape(-1)
    anchor_dims = lookup(left_dims, anchor)
    own_dims = lax.dynamic_slice_in_dim(right_dims, position * sectors, sectors, 0)
    out_keep = (indices[None, None, :, None] < anchor_dims[:, :, None, None]) & (
        indices[None, None, None, :] < own_dims[:, None, None, None]
    )
    products = jnp.stack(
        [
            jnp.einsum(
                "jxy,jpyz->jpxz", left_ops[term], masked, preferred_element_type=jnp.float32
            ).astype(jnp.bfloat16)
            for term in range(term_count)
        ]
    )
    flattened = products.reshape(term_count, item_count, block_width, block_width)
    outgoing = jnp.take(flattened, source_item, axis=1) * slot_used[None, :, None, None].astype(
        jnp.bfloat16
    )
    incoming = lax.all_to_all(outgoing, "sec", split_axis=1, concat_axis=1, tiled=True)
    arrived = jnp.take(incoming, gather_rows, axis=1).reshape(
        term_count, sectors, state_count, block_width, block_width
    )
    partial_value = jnp.zeros((sectors, state_count, block_width, block_width), jnp.float32)
    for term in range(term_count):
        partial_value = (
            partial_value
            + jnp.einsum(
                "jpxy,jyz->jpxz", arrived[term], right_ops[term], preferred_element_type=jnp.float32
            )
            * site_weights[term][None, :, None, None]
        )
    partial_value = jnp.where(out_keep, partial_value, 0.0)
    sigma_block = lax.psum_scatter(partial_value, "ops", scatter_dimension=2, tiled=True).astype(
        jnp.bfloat16
    )
    local_correlation = jnp.einsum(
        "vjpxy,jpxy->v", basis, sigma_block, preferred_element_type=jnp.float32
    )
    correlations = lax.psum(local_correlation, ("ops", "sec"))
    return (sigma_block, correlations)


def solution(mesh):
    in_specs = (
        P("sec", None, None, None),
        P("ops", "sec", None, None),
        P("ops", "sec", None, None),
        P("ops", None),
        P(),
        P(),
        P(),
        P(None, "sec", None, "ops", None),
    )
    out_specs = (P("sec", None, "ops", None), P())
    return jax.shard_map(
        per_device, mesh=mesh, in_specs=in_specs, out_specs=out_specs, check_vma=False
    )
```

profile of v0, /device:TPU:1, one launch (start us, length us, event | category | flops | bytes accessed | tf_op | source)
XLA Modules:
  0.0 505.0 jit_solution(2333832717340481551)
XLA Ops:
  7.2 0.0 copy-start
  7.2 0.8 add_select_fusion.1
  8.0 0.1 copy.60
  8.1 0.1 reshape.157
  8.2 0.1 copy.61
  8.3 2.3 fusion.3
  10.5 0.2 add_reduce_fusion
  10.7 0.1 select_reduce_fusion.4
  10.8 0.1 fusion.26
  11.0 0.8 constant_dynamic-slice_fusion
  11.7 0.8 dynamic_slice.17
  12.5 0.1 iota_compare_fusion.8
  12.6 0.1 copy.64
  12.6 0.9 select_reduce_fusion.1
  13.5 0.1 iota_compare_fusion.6
  13.6 0.0 copy-start.7
  13.6 0.0 copy-start.8
  13.6 2.9 convolution_convert_fusion.2
  16.6 0.0 copy-done.7
  16.6 0.0 copy-done.8
  16.6 1.2 convolution_convert_fusion.1
  17.8 1.2 convolution_convert_fusion
  19.0 1.2 convolution_convert_fusion.3
  20.3 3.8 pad_maximum_fusion
  24.1 8.9 %gather_fusion = bf16[64,4,128,128]{2,3,1,0:T(8,128)(2,1)} fusion(bf16[4,64,128,128]{2,3,1,0:T(8,128)(2,1)} %pad_maximum_fusion, s32[1024]{0:T(1024)S(1)} %pad_clamp_fusion.1), kind=kCustom, calls=%fused_computation.clone | custom fusion | bytes 16777472 | tf_op jit(solution)/shard_map/jit(_take)/gather | solution.py:69
  33.0 7.5 %bitcast_multiply_fusion = bf16[4,64,128,128]{2,3,0,1:T(8,128)(2,1)} fusion(bf16[64,4,128,128]{2,3,1,0:T(8,128)(2,1)} %gather_fusion, pred[64]{0:T(512)(128)(4,1)S(1)} %compare_and_fusion.1, bf16[64]{0:T(256)(128)(2,1)S(1)} %convert_element_type.47), kind=kLoop, calls=%fused_computation.3 | loop fusion | flops 8388608 | bytes 16777408 | tf_op jit(solution)/shard_map/mul | solution.py:69
  40.5 0.0 copy-start.5
  40.5 0.0 copy-start.3
  40.5 0.0 copy-start.6
  40.5 0.0 copy-start.4
  40.5 17.5 %all-to-all-start = ((bf16[4,64,128,128]{2,3,0,1:T(8,128)(2,1)}), bf16[4,64,128,128]{2,3,0,1:T(8,128)(2,1)}, u32[]{:S(2)}, u32[]{:S(2)}) async-start(bf16[4,64,128,128]{2,3,0,1:T(8,128)(2,1)} %bitcast_multiply_fusion), calls=%async_computation | async-start | bytes 16777216 | tf_op jit(solution)/shard_map/all_to_all | solution.py:72
  58.0 0.2 reduce-scatter.2.cloned.1.call-start
  58.3 0.0 copy-done.5
  58.3 0.1 dynamic_slice.16
  58.4 0.1 copy.62
  58.4 0.0 copy-done.3
  58.4 0.2 select_reduce_fusion.3
  58.7 0.1 reduce_sum.63
  58.7 0.1 reshape.158
  58.8 0.3 select_reduce_fusion
  59.2 0.1 reduce_sum.65
  59.3 0.0 copy-done.6
  59.3 0.2 select_reduce_fusion.2
  59.5 0.1 iota_compare_fusion.9
  59.6 0.0 copy-done.4
  59.6 0.1 iota_compare_fusion.7
  59.7 254.2 %all-to-all-done = bf16[4,64,128,128]{2,3,0,1:T(8,128)(2,1)} async-done(((bf16[4,64,128,128]{2,3,0,1:T(8,128)(2,1)}), bf16[4,64,128,128]{2,3,0,1:T(8,128)(2,1)}, u32[]{:S(2)}, u32[]{:S(2)}) %all-to-all-start) | async-done | bytes 8388640 | tf_op jit(solution)/shard_map/all_to_all | solution.py:72
  313.9 8.9 %gather_fusion.1 = bf16[64,4,128,128]{2,3,1,0:T(8,128)(2,1)} fusion(bf16[4,64,128,128]{2,3,0,1:T(8,128)(2,1)} %all-to-all-done, s32[1024]{0:T(1024)S(1)} %pad_clamp_fusion), kind=kCustom, calls=%fused_computation.1.clone | custom fusion | bytes 16777472 | tf_op jit(solution)/shard_map/jit(_take)/gather | solution.py:73
  322.8 7.5 %select_bitcast_fusion = bf16[4,64,128,128]{2,3,0,1:T(8,128)(2,1)} fusion(bf16[64,4,128,128]{2,3,1,0:T(8,128)(2,1)} %gather_fusion.1, pred[64]{0:T(512)(128)(4,1)S(1)} %get-tuple-element.3), kind=kLoop, calls=%fused_computation.4 | loop fusion | flops 4194304 | bytes 16777280 | tf_op jit(solution)/shard_map/jit(_take)/select_n | solution.py:73
  330.3 3.9 fusion.39
  334.2 0.0 copy-done.2
  334.2 0.9 fusion.8
  335.1 0.9 fusion.10
  336.0 0.9 fusion.12
  336.9 5.0 add_select_fusion
  341.9 0.0 reduce-scatter.2.cloned.1.call-update
  341.9 52.5 %reduce-scatter.2.cloned.1.call-done = f32[4,16,16,128]{3,2,1,0:T(8,128)} async-done(((f32[4,16,128,128]{3,2,1,0:T(8,128)}), f32[4,16,16,128]{3,2,1,0:T(8,128)}) %reduce-scatter.2.cloned.1.call-update) | async-done | bytes 524304 | tf_op jit(solution)/shard_map/reduce_scatter | solution.py:86
  394.4 1.1 convert_bitcast_fusion
  395.5 0.0 copy-done
  395.5 0.0 copy-start.1
  395.5 1.6 convolution_bitcast_fusion
  397.1 100.3 %psum.7 = f32[4]{0:T(128)} all-reduce(f32[4]{0:T(128)S(1)} %convolution_bitcast_fusion), channel_id=1, replica_groups=mesh['ops'=8,'sec'=64] {'ops','sec'}, use_global_device_ids=true, to_apply=%region_9.11 | all-reduce | flops 4 | bytes 32 | tf_op jit(solution)/shard_map/psum | solution.py:92
  497.4 0.0 copy-done.1
  497.4 0.7 convert_element_type.48
  (10 shorter events, 0.1 us)
Async XLA Ops:
  7.2 388.3 %copy-start = (bf16[4,4,16,16,128]{4,3,2,1,0:T(8,128)(2,1)S(1)}, bf16[4,4,16,16,128]{4,3,2,1,0:T(8,128)(2,1)}, u32[]{:S(2)}) copy-start(bf16[4,4,16,16,128]{4,3,2,1,0:T(8,128)(2,1)} %param.17) | copy-start | bytes 3145732
  13.6 3.0 copy-start.7
  13.6 3.0 copy-start.8
  40.5 17.8 %copy-start.5 = (s32[256]{0:T(256)S(1)}, s32[256]{0:T(256)}, u32[]{:S(2)}) copy-start(s32[256]{0:T(256)} %param.16) | copy-start | bytes 3076
  40.5 18.0 %copy-start.3 = (s32[256,16]{0,1:T(8,128)S(1)}, s32[256,16]{0,1:T(8,128)}, u32[]{:S(2)}) copy-start(s32[256,16]{0,1:T(8,128)} %param.14) | copy-start | bytes 49156
  40.5 18.8 %copy-start.6 = (s32[256]{0:T(256)S(1)}, s32[256]{0:T(256)}, u32[]{:S(2)}) copy-start(s32[256]{0:T(256)} %param.15) | copy-start | bytes 3076
  40.5 19.1 %copy-start.4 = (f32[4,16]{1,0:T(4,128)S(1)}, f32[4,16]{1,0:T(4,128)}, u32[]{:S(2)}) copy-start(f32[4,16]{1,0:T(4,128)} %param.13) | copy-start | bytes 772
  40.5 273.4 %all-to-all-start = ((bf16[4,64,128,128]{2,3,0,1:T(8,128)(2,1)}), bf16[4,64,128,128]{2,3,0,1:T(8,128)(2,1)}, u32[]{:S(2)}, u32[]{:S(2)}) async-start(bf16[4,64,128,128]{2,3,0,1:T(8,128)(2,1)} %bitcast_multiply_fusion), calls=%async_computation | async-start | bytes 16777216 | tf_op jit(solution)/shard_map/all_to_all | solution.py:72
  58.0 336.4 %reduce-scatter.2.cloned.1.call-start = ((), (), s32[]{:S(2)}) async-start(), calls=%async_computation.2 | async-start | bytes 4718592 | tf_op jit(solution)/shard_map/reduce_scatter | solution.py:86
  330.3 4.0 copy-start.2
  395.5 102.0 %copy-start.1 = (f32[4,16,16,128]{3,2,1,0:T(8,128)S(1)}, f32[4,16,16,128]{3,2,1,0:T(8,128)}, u32[]{:S(2)}) copy-start(f32[4,16,16,128]{3,2,1,0:T(8,128)} %reduce-scatter.2.cloned.1.call-done) | copy-start | bytes 1572868
Sparse Core Ops, SparseCore 0:
  342.1 52.2 reduce-scatter.1
where the time goes:
time: 506 us; the launch traced here: 505 us
  waiting for transfers between devices  307 us (61%)
  blocking collectives  100 us (20%)
  other arithmetic  26 us (5%)
  local copies, waits for them, and re-layouts  24.1 us (5%)
  starting transfers between devices  17.8 us (4%)
  matrix products  15.9 us (3%)
  between operations  14.3 us (3%)
    all_to_all x1, waiting for transfers between devices, per_device(): lax.all_to_all(outgoing, 'sec', split_axis=1, concat_axis=1, tiled=True)  254 us
    psum x1, blocking collectives, per_device(): correlations = lax.psum(local_correlation, ('ops', 'sec'))  100 us
    reduce_scatter x1, waiting for transfers between devices, per_device(): lax.psum_scatter(partial_value, 'ops', scatter_dimension=2, tiled=True)  52.5 us
    all_to_all x1, starting transfers between devices, per_device(): lax.all_to_all(outgoing, 'sec', split_axis=1, concat_axis=1, tiled=True)  17.5 us
  transfers between devices with their start and end apart: 2, of which 2 were waited for; matrix products, arithmetic and copies ran while one was open for 0% of the time, Pallas kernels for 0%

commit v1 on v0

--- a/solution.py
+++ b/solution.py
@@ -89,7 +89,9 @@
     local_correlation = jnp.einsum(
         "vjpxy,jpxy->v", basis, sigma_block, preferred_element_type=jnp.float32
     )
-    correlations = lax.psum(local_correlation, ("ops", "sec"))
+    correlations = local_correlation
+    for dd in ("sec", "ops"):
+        correlations = lax.psum(correlations, dd)
     return (sigma_block, correlations)
 
 

time: 506 us -> 565 us (1.12)
  blocking collectives: 100 us -> 159 us
    psum x1 -> x2, blocking collectives: 100 us -> 159 us  [per_device(): correlations = lax.psum(correlations, dd)]
where the time goes in v1:
time: 565 us; the launch traced here: 564 us
  waiting for transfers between devices  307 us (54%)
  blocking collectives  159 us (28%)
  other arithmetic  26 us (5%)
  local copies, waits for them, and re-layouts  24.1 us (4%)
  starting transfers between devices  17.8 us (3%)
  matrix products  15.9 us (3%)
  between operations  14.3 us (3%)
    all_to_all x1, waiting for transfers between devices, per_device(): lax.all_to_all(outgoing, 'sec', split_axis=1, concat_axis=1, tiled=True)  254 us
    psum x2, blocking collectives, per_device(): correlations = lax.psum(correlations, dd)  159 us
    reduce_scatter x1, waiting for transfers between devices, per_device(): lax.psum_scatter(partial_value, 'ops', scatter_dimension=2, tiled=True)  52.5 us
    all_to_all x1, starting transfers between devices, per_device(): lax.all_to_all(outgoing, 'sec', split_axis=1, concat_axis=1, tiled=True)  17.5 us
  transfers between devices with their start and end apart: 2, of which 2 were waited for; matrix products, arithmetic and copies ran while one was open for 0% of the time, Pallas kernels for 0%

profile of v1, /device:TPU:1, one launch (start us, length us, event | category | flops | bytes accessed | tf_op | source)
XLA Modules:
  0.0 564.2 jit_solution(340102954706253573)
XLA Ops:
  7.2 0.0 copy-start
  7.2 0.8 add_select_fusion.1
  8.0 0.1 copy.60
  8.1 0.1 reshape.157
  8.2 0.1 copy.61
  8.3 2.3 fusion.3
  10.5 0.2 add_reduce_fusion
  10.7 0.1 select_reduce_fusion.4
  10.8 0.1 fusion.26
  11.0 0.8 constant_dynamic-slice_fusion
  11.7 0.8 dynamic_slice.17
  12.5 0.1 iota_compare_fusion.8
  12.6 0.1 copy.64
  12.6 0.9 select_reduce_fusion.1
  13.5 0.1 iota_compare_fusion.6
  13.6 0.0 copy-start.7
  13.6 0.0 copy-start.8
  13.6 2.9 convolution_convert_fusion.2
  16.6 0.0 copy-done.7
  16.6 0.0 copy-done.8
  16.6 1.2 convolution_convert_fusion.1
  17.8 1.2 convolution_convert_fusion
  19.0 1.2 convolution_convert_fusion.3
  20.3 3.8 pad_maximum_fusion
  24.1 8.9 %gather_fusion = bf16[64,4,128,128]{2,3,1,0:T(8,128)(2,1)} fusion(bf16[4,64,128,128]{2,3,1,0:T(8,128)(2,1)} %pad_maximum_fusion, s32[1024]{0:T(1024)S(1)} %pad_clamp_fusion.1), kind=kCustom, calls=%fused_computation.clone | custom fusion | bytes 16777472 | tf_op jit(solution)/shard_map/jit(_take)/gather | solution.py:69
  33.0 7.5 %bitcast_multiply_fusion = bf16[4,64,128,128]{2,3,0,1:T(8,128)(2,1)} fusion(bf16[64,4,128,128]{2,3,1,0:T(8,128)(2,1)} %gather_fusion, pred[64]{0:T(512)(128)(4,1)S(1)} %compare_and_fusion.1, bf16[64]{0:T(256)(128)(2,1)S(1)} %convert_element_type.47), kind=kLoop, calls=%fused_computation.3 | loop fusion | flops 8388608 | bytes 16777408 | tf_op jit(solution)/shard_map/mul | solution.py:69
  40.5 0.0 copy-start.5
  40.5 0.0 copy-start.3
  40.5 0.0 copy-start.6
  40.5 17.5 %all-to-all-start = ((bf16[4,64,128,128]{2,3,0,1:T(8,128)(2,1)}), bf16[4,64,128,128]{2,3,0,1:T(8,128)(2,1)}, u32[]{:S(2)}, u32[]{:S(2)}) async-start(bf16[4,64,128,128]{2,3,0,1:T(8,128)(2,1)} %bitcast_multiply_fusion), calls=%async_computation | async-start | bytes 16777216 | tf_op jit(solution)/shard_map/all_to_all | solution.py:72
  58.0 0.2 reduce-scatter.2.cloned.1.call-start
  58.3 0.0 copy-done.5
  58.3 0.1 dynamic_slice.16
  58.4 0.1 copy.62
  58.4 0.0 copy-done.3
  58.4 0.2 select_reduce_fusion.3
  58.7 0.1 reduce_sum.63
  58.7 0.1 reshape.158
  58.8 0.3 select_reduce_fusion
  59.2 0.1 reduce_sum.65
  59.3 0.0 copy-done.6
  59.3 0.2 select_reduce_fusion.2
  59.5 0.1 iota_compare_fusion.9
  59.6 0.0 copy-done.4
  59.6 0.1 iota_compare_fusion.7
  59.7 254.2 %all-to-all-done = bf16[4,64,128,128]{2,3,0,1:T(8,128)(2,1)} async-done(((bf16[4,64,128,128]{2,3,0,1:T(8,128)(2,1)}), bf16[4,64,128,128]{2,3,0,1:T(8,128)(2,1)}, u32[]{:S(2)}, u32[]{:S(2)}) %all-to-all-start) | async-done | bytes 8388640 | tf_op jit(solution)/shard_map/all_to_all | solution.py:72
  313.9 8.9 %gather_fusion.1 = bf16[64,4,128,128]{2,3,1,0:T(8,128)(2,1)} fusion(bf16[4,64,128,128]{2,3,0,1:T(8,128)(2,1)} %all-to-all-done, s32[1024]{0:T(1024)S(1)} %pad_clamp_fusion), kind=kCustom, calls=%fused_computation.1.clone | custom fusion | bytes 16777472 | tf_op jit(solution)/shard_map/jit(_take)/gather | solution.py:73
  322.8 7.5 %select_bitcast_fusion = bf16[4,64,128,128]{2,3,0,1:T(8,128)(2,1)} fusion(bf16[64,4,128,128]{2,3,1,0:T(8,128)(2,1)} %gather_fusion.1, pred[64]{0:T(512)(128)(4,1)S(1)} %get-tuple-element.3), kind=kLoop, calls=%fused_computation.4 | loop fusion | flops 4194304 | bytes 16777280 | tf_op jit(solution)/shard_map/jit(_take)/select_n | solution.py:73
  330.3 3.9 fusion.39
  334.2 0.0 copy-done.2
  334.2 0.9 fusion.8
  335.1 0.9 fusion.10
  336.0 0.9 fusion.12
  336.9 5.0 add_select_fusion
  341.9 0.0 reduce-scatter.2.cloned.1.call-update
  341.9 52.5 %reduce-scatter.2.cloned.1.call-done = f32[4,16,16,128]{3,2,1,0:T(8,128)} async-done(((f32[4,16,128,128]{3,2,1,0:T(8,128)}), f32[4,16,16,128]{3,2,1,0:T(8,128)}) %reduce-scatter.2.cloned.1.call-update) | async-done | bytes 524304 | tf_op jit(solution)/shard_map/reduce_scatter | solution.py:86
  394.4 1.1 convert_bitcast_fusion
  395.5 0.0 copy-done
  395.5 0.0 copy-start.1
  395.5 1.6 convolution_bitcast_fusion
  397.1 116.0 %psum.14 = f32[4]{0:T(128)S(1)} all-reduce(f32[4]{0:T(128)S(1)} %convolution_bitcast_fusion), channel_id=1, replica_groups=mesh['ops'=8,'sec'=64] {'sec'}, use_global_device_ids=true, to_apply=%region_9.11 | all-reduce | flops 4 | bytes 32 | tf_op jit(solution)/shard_map/psum | solution.py:94
  513.2 43.4 %psum.15 = f32[4]{0:T(128)} all-reduce(f32[4]{0:T(128)S(1)} %psum.14), channel_id=1, replica_groups=mesh['ops'=8,'sec'=64] {'ops'}, use_global_device_ids=true, to_apply=%region_10.12 | all-reduce | flops 4 | bytes 32 | tf_op jit(solution)/shard_map/psum | solution.py:94
  556.6 0.0 copy-done.1
  556.6 0.7 convert_element_type.48
  (11 shorter events, 0.1 us)
Async XLA Ops:
  7.2 388.3 %copy-start = (bf16[4,4,16,16,128]{4,3,2,1,0:T(8,128)(2,1)S(1)}, bf16[4,4,16,16,128]{4,3,2,1,0:T(8,128)(2,1)}, u32[]{:S(2)}) copy-start(bf16[4,4,16,16,128]{4,3,2,1,0:T(8,128)(2,1)} %param.17) | copy-start | bytes 3145732
  13.6 3.0 copy-start.7
  13.6 3.0 copy-start.8
  40.5 17.8 %copy-start.5 = (s32[256]{0:T(256)S(1)}, s32[256]{0:T(256)}, u32[]{:S(2)}) copy-start(s32[256]{0:T(256)} %param.16) | copy-start | bytes 3076
  40.5 18.0 %copy-start.3 = (s32[256,16]{0,1:T(8,128)S(1)}, s32[256,16]{0,1:T(8,128)}, u32[]{:S(2)}) copy-start(s32[256,16]{0,1:T(8,128)} %param.14) | copy-start | bytes 49156
  40.5 18.8 %copy-start.6 = (s32[256]{0:T(256)S(1)}, s32[256]{0:T(256)}, u32[]{:S(2)}) copy-start(s32[256]{0:T(256)} %param.15) | copy-start | bytes 3076
  40.5 19.1 %copy-start.4 = (f32[4,16]{1,0:T(4,128)S(1)}, f32[4,16]{1,0:T(4,128)}, u32[]{:S(2)}) copy-start(f32[4,16]{1,0:T(4,128)} %param.13) | copy-start | bytes 772
  40.5 273.4 %all-to-all-start = ((bf16[4,64,128,128]{2,3,0,1:T(8,128)(2,1)}), bf16[4,64,128,128]{2,3,0,1:T(8,128)(2,1)}, u32[]{:S(2)}, u32[]{:S(2)}) async-start(bf16[4,64,128,128]{2,3,0,1:T(8,128)(2,1)} %bitcast_multiply_fusion), calls=%async_computation | async-start | bytes 16777216 | tf_op jit(solution)/shard_map/all_to_all | solution.py:72
  58.0 336.4 %reduce-scatter.2.cloned.1.call-start = ((), (), s32[]{:S(2)}) async-start(), calls=%async_computation.2 | async-start | bytes 4718592 | tf_op jit(solution)/shard_map/reduce_scatter | solution.py:86
  330.3 4.0 copy-start.2
  395.5 161.1 %copy-start.1 = (f32[4,16,16,128]{3,2,1,0:T(8,128)S(1)}, f32[4,16,16,128]{3,2,1,0:T(8,128)}, u32[]{:S(2)}) copy-start(f32[4,16,16,128]{3,2,1,0:T(8,128)} %reduce-scatter.2.cloned.1.call-done) | copy-start | bytes 1572868
Sparse Core Ops, SparseCore 0:
  342.1 52.2 reduce-scatter.1
